TPU v7x, 32 devices: a whole 2x2x4 slice. The times are simulated.
32 devices in a mesh: resp: 16 (over z, y, x), head: 2 (over core).
Axes of the slice: x: 2, y: 2, z: 4, core: 2. Of those that a mesh axis runs over, the one named last changes fastest.
Arguments:
- queries: bfloat16 [2048, 24576], P('resp', 'head'), may hold values from -8 to 8
- resp_latent: bfloat16 [2048, 576], P('resp'), may hold values from -8 to 8
- prompt_latent: bfloat16 [16, 32, 576], P('resp'), may hold values from -6 to 6
- up_keys: bfloat16 [128, 128, 512], P('head', None, 'resp'), may hold values from -0.5 to 0.5
- up_values: bfloat16 [128, 512, 128], P('head', 'resp'), may hold values from -0.25 to 0.25
- cotangent: bfloat16 [2048, 16384], P('resp', 'head'), may hold values from -6 to 6
- prompt_len: int32 [8], replicated, may hold values from 8 to 32
- resp_len: int32 [32], replicated, may hold values from 16 to 64
- resp_count: int32 [8], replicated, may hold values from 1 to 8, 32 in all
- owner: int32 [8], replicated, may hold values from 0 to 15, as said below
Outputs:
- attended: bfloat16 [2048, 16384], P('resp', 'head')
- grad_queries: bfloat16 [2048, 24576], P('resp', 'head')
- grad_response: float32 [2048, 576], P('resp', 'head')
- grad_prompt: float32 [16, 32, 576], P('resp', None, 'head')
Inputs may be any that keep to these rules, and one draw needn't show every extreme that they name: Distinct slots; prompt p's cache is prompt_latent[owner[p]]. `resp_count`: every prompt has at least one response; they sum to 32.
All inputs are finite; a program needn't handle non-finite values.
Results may differ from a plain program's by a relative error of at most 0.014.
Values may be sent and summed in bfloat16 or wider, within the bound.
A program may use at most 128 MiB of HBM per device.

v0:
```python
import functools
import math

import jax
import jax.numpy as jnp
from jax import lax
from jax.experimental import pallas as pl
from jax.experimental.pallas import tpu as pltpu
from jax.sharding import PartitionSpec as P

MESH = pl.DeviceIdType.MESH
NT = (((1,), (1,)), ((), ()))
NN = (((1,), (0,)), ((), ()))
TN = (((0,), (0,)), ((), ()))


def mm(left, right, form):
    return lax.dot_general(left, right, form, preferred_element_type=jnp.float32)


def kernel(
    line,
    chunks,
    heads_per,
    resp_per,
    meta,
    q_ref,
    cot_ref,
    w_ref,
    prompt_ref,
    resp_ref,
    att_ref,
    gq_ref,
    gk_ref,
    full,
    prompts,
    keys,
    qf,
    gl,
    lo,
    gf,
    own_sem,
    line_send,
    line_recv,
    pair_send,
    pair_recv,
):
    step = pl.program_id(0)
    me = lax.axis_index("resp")
    x = lax.rem(me, 2)
    y = lax.rem(lax.div(me, 2), 2)
    z = lax.div(me, 4)

    def at(zz, yy, xx):
        return {"resp": (zz * 2 + yy) * 2 + xx}

    y_peer, x_peer = at(z, 1 - y, x), at(z, y, 1 - x)

    def remote(src, dst, send, recv, peer):
        return pltpu.make_async_remote_copy(
            src_ref=src, dst_ref=dst, send_sem=send, recv_sem=recv, device_id=peer, device_id_type=MESH
        )

    def heads(c):
        return pl.ds(c * heads_per, heads_per)

    def own_copy(c):
        return pltpu.make_async_copy(
            w_ref.at[:, heads(c)], full.at[:, z, y, x, heads(c)], own_sem.at[c]
        )

    def line_copy(c, d, source):
        return remote(
            w_ref.at[:, heads(c)],
            full.at[:, source, y, x, heads(c)],
            line_send.at[c, d - 1],
            line_recv.at[c, d - 1],
            at(lax.rem(z + d, line), y, x),
        )

    def pair_copies(c, yy, xx):
        first_k = full.at[0, :, yy[0], xx[0], heads(c)]
        first_v = full.at[1, :, yy[1], xx[1], heads(c)]
        second_k = full.at[0, :, :, xx[2], heads(c)]
        second_v = full.at[1, :, yy[2], :, heads(c)]
        refs = ((first_k, y_peer), (first_v, x_peer), (second_k, x_peer), (second_v, y_peer))
        return [
            remote(ref, ref, pair_send.at[c, i], pair_recv.at[c, i], peer)
            for i, (ref, peer) in enumerate(refs)
        ]

    def out_pairs(c):
        return pair_copies(c, (y, y, y), (x, x, x))

    def in_pairs(c):
        return pair_copies(c, (1 - y, y, 1 - y), (x, 1 - x, 1 - x))

    def own_prompt():
        return pltpu.make_async_copy(prompt_ref.at[0], prompts.at[z, y, x], own_sem.at[chunks])

    def line_prompt(d, source):
        return remote(
            prompt_ref.at[0],
            prompts.at[source, y, x],
            line_send.at[chunks, d - 1],
            line_recv.at[chunks, d - 1],
            at(lax.rem(z + d, line), y, x),
        )

    def prompt_pairs(yy, xx):
        refs = ((prompts.at[:, yy, x], y_peer), (prompts.at[:, :, xx], x_peer))
        return [
            remote(ref, ref, pair_send.at[chunks, i], pair_recv.at[chunks, i], peer)
            for i, (ref, peer) in enumerate(refs)
        ]

    @pl.when(step == 0)
    def _():
        barrier = pltpu.get_barrier_semaphore()
        for d in range(1, line):
            pl.semaphore_signal(
                barrier, inc=1, device_id=at(lax.rem(z + d, line), y, x), device_id_type=MESH
            )
        pl.semaphore_signal(barrier, inc=1, device_id=y_peer, device_id_type=MESH)
        pl.semaphore_signal(barrier, inc=1, device_id=x_peer, device_id_type=MESH)
        pl.semaphore_wait(barrier, line + 1)
        own_prompt().start()
        for d in range(1, line):
            line_prompt(d, z).start()
        gk_ref[...] = jnp.zeros_like(gk_ref)

    @pl.when(step < chunks)
    def _():
        own_copy(step).start()
        for d in range(1, line):
            line_copy(step, d, z).start()

    @pl.when(step == 1)
    def _():
        own_prompt().wait()
        for d in range(1, line):
            line_prompt(d, lax.rem(z + line - d, line)).wait_recv()
        prompt_pairs(y, x)[0].start()

    @pl.when((step >= 1) & (step < chunks + 1))
    def _():
        c = step - 1
        own_copy(c).wait()
        for d in range(1, line):
            line_copy(c, d, lax.rem(z + line - d, line)).wait_recv()
        sends = out_pairs(c)
        sends[0].start()
        sends[1].start()

    @pl.when(step == 2)
    def _():
        prompt_pairs(1 - y, 1 - x)[0].wait_recv()
        prompt_pairs(y, x)[1].start()

    @pl.when((step >= 2) & (step < chunks + 2))
    def _():
        c = step - 2
        arrivals, sends = in_pairs(c), out_pairs(c)
        arrivals[0].wait_recv()
        arrivals[1].wait_recv()
        sends[2].start()
        sends[3].start()

    plen_rows = prompt_ref.shape[1]
    tokens = resp_ref.shape[1]
    key_count, key_cols = keys.shape[1], keys.shape[2]
    latent = gl.shape[2]
    slice_cols, nope = w_ref.shape[2], w_ref.shape[3]
    value_cols = nope
    q_cols = q_ref.shape[1] // heads_per
    rows = heads_per * tokens
    scale = 1.0 / math.sqrt(q_cols)

    @pl.when(step == 3)
    def _():
        prompt_pairs(1 - y, 1 - x)[1].wait_recv()
        for r in range(resp_per):
            keys[r, :plen_rows, :] = prompts[meta[r, 0], meta[r, 1], meta[r, 2]]
            keys[r, plen_rows:, :] = resp_ref[r]

    @pl.when(step >= 3)
    def _():
        c = step - 3
        arrivals = in_pairs(c)
        arrivals[2].wait_recv()
        arrivals[3].wait_recv()

        def weight(kind, h):
            got = full[kind, :, :, :, c * heads_per + h]
            if slice_cols % 16:
                return got.astype(jnp.float32).reshape(latent, nope).astype(jnp.bfloat16)
            return got.reshape(latent, nope)

        token_row = lax.broadcasted_iota(jnp.int32, (resp_per * tokens, 1), 0)
        live = jnp.zeros((resp_per * tokens, 1), jnp.float32)
        for r in range(resp_per):
            inside = (token_row >= r * tokens) & (token_row < r * tokens + meta[r, 4])
            live = jnp.where(inside, 1.0, live)

        for h in range(heads_per):
            wk, wv = weight(0, h), weight(1, h)
            q_latent = mm(q_ref[:, h * q_cols : h * q_cols + nope], wk, NT).astype(jnp.bfloat16)
            rope = q_ref[:, h * q_cols + nope : (h + 1) * q_cols]
            grad_latent = mm(cot_ref[:, h * value_cols : (h + 1) * value_cols], wv, NT) * live
            grad_latent = grad_latent.astype(jnp.bfloat16)
            for r in range(resp_per):
                mine = slice(r * tokens, (r + 1) * tokens)
                place = slice(h * tokens, (h + 1) * tokens)
                qf[r, place, :latent] = q_latent[mine]
                qf[r, place, latent:] = rope[mine]
                gl[r, place, :] = grad_latent[mine]

        key_at = lax.broadcasted_iota(jnp.int32, (key_count, rows), 0)
        token_at = lax.rem(lax.broadcasted_iota(jnp.int32, (key_count, rows), 1), tokens)
        for r in range(resp_per):
            key = keys[r]
            value = key[:, :latent]
            query, grad_latent = qf[r], gl[r]
            scores = mm(key, query, NT) * scale
            last = jnp.where(key_at < plen_rows, meta[r, 3] - 1, token_at + plen_rows)
            scores = jnp.where(key_at <= last, scores, -jnp.inf)
            expo = jnp.exp(scores - jnp.max(scores, axis=0, keepdims=True))
            weights = expo / jnp.sum(expo, axis=0, keepdims=True)
            weights_bf = weights.astype(jnp.bfloat16)
            grad_weights = mm(value, grad_latent, NT)
            inner = jnp.sum(weights * grad_weights, axis=0, keepdims=True)
            grad_scores = (weights * (grad_weights - inner) * scale).astype(jnp.bfloat16)
            lo_r = mm(weights_bf, value, TN).astype(jnp.bfloat16)
            gf_r = mm(grad_scores, key, TN).astype(jnp.bfloat16)
            for h in range(heads_per):
                mine = slice(r * tokens, (r + 1) * tokens)
                place = slice(h * tokens, (h + 1) * tokens)
                lo[h, mine, :] = lo_r[place]
                gf[h, mine, :] = gf_r[place]
            gk_ref[r] += mm(grad_scores, query, NN)
            gk_ref[r, :, :latent] += mm(weights_bf, grad_latent, NN)

        for h in range(heads_per):
            wk, wv = weight(0, h), weight(1, h)
            attended = mm(lo[h], wv, NN) * live
            att_ref[:, h * value_cols : (h + 1) * value_cols] = attended.astype(jnp.bfloat16)
            grad_nope = mm(gf[h, :, :latent], wk, NN).astype(jnp.bfloat16)
            gq_ref[:, h * q_cols : h * q_cols + nope] = grad_nope
            gq_ref[:, h * q_cols + nope : (h + 1) * q_cols] = gf[h, :, latent:]

        sends = out_pairs(c)
        for i in range(4):
            sends[i].wait_send()
        for d in range(1, line):
            line_copy(c, d, z).wait_send()

    @pl.when(step == 3)
    def _():
        sends = prompt_pairs(y, x)
        sends[0].wait_send()
        sends[1].wait_send()
        for d in range(1, line):
            line_prompt(d, z).wait_send()


def fused(queries, cotangent, weights, prompt_latent, own_rows, meta, resp_devices):
    line = resp_devices // 4
    head_count, slice_cols, nope = weights.shape[1:]
    resp_per, tokens, key_cols = own_rows.shape
    prompt_rows = prompt_latent.shape[1]
    heads_per = math.gcd(4, head_count)
    chunks = head_count // heads_per
    row_count = queries.shape[0]
    q_cols = queries.shape[1] // head_count
    latent = slice_cols * resp_devices
    key_count = prompt_rows + tokens
    rows = heads_per * tokens
    bf = jnp.bfloat16

    def tile(t):
        return (0, lax.max(t - 3, 0))

    whole = pl.BlockSpec(memory_space=pltpu.VMEM)
    return pl.pallas_call(
        functools.partial(kernel, line, chunks, heads_per, resp_per),
        out_shape=(
            jax.ShapeDtypeStruct(cotangent.shape, bf),
            jax.ShapeDtypeStruct(queries.shape, bf),
            jax.ShapeDtypeStruct((resp_per, key_count, key_cols), jnp.float32),
        ),
        grid=(chunks + 3,),
        in_specs=[
            pl.BlockSpec(memory_space=pltpu.SMEM),
            pl.BlockSpec((row_count, heads_per * q_cols), tile),
            pl.BlockSpec((row_count, heads_per * nope), tile),
            whole,
            whole,
            whole,
        ],
        out_specs=(
            pl.BlockSpec((row_count, heads_per * nope), tile),
            pl.BlockSpec((row_count, heads_per * q_cols), tile),
            whole,
        ),
        scratch_shapes=[
            pltpu.VMEM((2, line, 2, 2, head_count, slice_cols, nope), bf),
            pltpu.VMEM((line, 2, 2, prompt_rows, key_cols), bf),
            pltpu.VMEM((resp_per, key_count, key_cols), bf),
            pltpu.VMEM((resp_per, rows, key_cols), bf),
            pltpu.VMEM((resp_per, rows, latent), bf),
            pltpu.VMEM((heads_per, resp_per * tokens, latent), bf),
            pltpu.VMEM((heads_per, resp_per * tokens, key_cols), bf),
            pltpu.SemaphoreType.DMA((chunks + 1,)),
            pltpu.SemaphoreType.DMA((chunks + 1, line - 1)),
            pltpu.SemaphoreType.DMA((chunks + 1, line - 1)),
            pltpu.SemaphoreType.DMA((chunks + 1, 4)),
            pltpu.SemaphoreType.DMA((chunks + 1, 4)),
        ],
        compiler_params=pltpu.CompilerParams(
            collective_id=0, has_side_effects=True, dimension_semantics=("arbitrary",)
        ),
    )(meta, queries, cotangent, weights, prompt_latent, own_rows)


def body(
    queries,
    resp_latent,
    prompt_latent,
    up_keys,
    up_values,
    cotangent,
    prompt_len,
    resp_len,
    resp_count,
    owner,
):
    resp_devices = lax.axis_size("resp")
    head_devices = lax.axis_size("head")
    my_index = lax.axis_index("resp")
    resp_total = resp_len.shape[0]
    per_device = resp_total // resp_devices
    row_count = queries.shape[0] // per_device
    prompt_rows = prompt_latent.shape[1]
    piece_rows = prompt_rows // resp_devices
    latent_cols = prompt_latent.shape[2]
    starts = jnp.cumsum(resp_count) - resp_count
    numbers = jnp.arange(resp_total, dtype=jnp.int32)
    prompt_of = jnp.sum((starts[None, :] <= numbers[:, None]).astype(jnp.int32), axis=1) - 1
    chosen = prompt_of[:, None] == jnp.arange(prompt_len.shape[0], dtype=jnp.int32)[None, :]
    slot_of = jnp.sum(jnp.where(chosen, owner[None, :], 0), axis=1)
    plen_of = jnp.sum(jnp.where(chosen, prompt_len[None, :], 0), axis=1)
    table = jnp.stack([slot_of // 4, (slot_of // 2) % 2, slot_of % 2, plen_of, resp_len], axis=1)
    meta = lax.dynamic_slice_in_dim(table, my_index * per_device, per_device)
    weights = jnp.stack([jnp.swapaxes(up_keys, 1, 2), up_values])
    own_rows = resp_latent.reshape(per_device, row_count, latent_cols)
    attended, grad_query, grad_key = fused(
        queries, cotangent, weights, prompt_latent, own_rows, meta, resp_devices
    )
    share = latent_cols // head_devices
    parts = grad_key.reshape(per_device, prompt_rows + row_count, head_devices, share)
    parts = jnp.moveaxis(parts, 2, 0).astype(jnp.bfloat16)
    parts = lax.all_to_all(parts, "head", split_axis=0, concat_axis=0, tiled=True)
    mine = jnp.sum(parts.astype(jnp.float32), axis=0)
    grad_own = mine[:, prompt_rows:].reshape(per_device * row_count, share)
    grad_prompt_rows = mine[:, :prompt_rows].astype(jnp.bfloat16)
    arrived = lax.all_to_all(
        grad_prompt_rows[None], "resp", split_axis=2, concat_axis=0, tiled=True
    ).astype(jnp.float32)
    flat_rows = arrived.reshape(resp_devices * per_device, piece_rows * share)
    slot_table = (slot_of[None, :] == jnp.arange(resp_devices, dtype=jnp.int32)[:, None]).astype(
        jnp.float32
    )
    summed = jnp.dot(slot_table, flat_rows, precision=lax.Precision.HIGHEST)
    summed = summed.reshape(resp_devices, piece_rows, share)
    at_owner = lax.all_to_all(
        summed.astype(jnp.bfloat16), "resp", split_axis=0, concat_axis=1, tiled=True
    ).astype(summed.dtype)
    return attended, grad_query, grad_own, at_owner


def solution(mesh):
    placed = (
        P("resp", "head"),
        P("resp", None),
        P("resp", None, None),
        P("head", None, "resp"),
        P("head", "resp", None),
        P("resp", "head"),
        P(),
        P(),
        P(),
        P(),
    )
    return jax.shard_map(
        body,
        mesh=mesh,
        in_specs=placed,
        out_specs=(
            P("resp", "head"),
            P("resp", "head"),
            P("resp", "head"),
            P("resp", None, "head"),
        ),
        check_vma=False,
    )
```

profile of v0, /device:TPU:0, one launch (start us, length us, event | category | flops | bytes accessed | tf_op | source)
XLA Modules:
  0.0 213.9 jit_solution(17802674593799246931)
XLA Ops:
  0.6 0.8 reduce-window.9
  1.5 0.7 bitcast_subtract_fusion
  2.1 0.1 convert_reduce_fusion.1
  2.2 0.8 select_reduce_fusion
  3.0 0.7 stack.23
  3.7 0.1 constant_dynamic-slice_fusion
  3.7 0.7 copy.52.meta
  4.4 1.7 copy.43
  6.1 2.3 %pad_maximum_fusion.w_ref = bf16[2,64,32,128]{3,2,1,0:T(8,128)(2,1)} fusion(bf16[1,64,32,128]{3,2,1,0:T(8,128)(2,1)} %bitcast.50, bf16[1,64,32,128]{3,2,1,0:T(8,128)(2,1)} %bitcast.51), kind=kLoop, calls=%fused_computation.1 | loop fusion | flops 524288 | bytes 2097152 | tf_op jit(solution)/shard_map/stack | solution.py:354
  8.4 168.8 %shard_map.129 = (bf16[128,8192]{1,0:T(8,128)(2,1)}, bf16[128,12288]{1,0:T(8,128)(2,1)}, f32[2,96,576]{2,1,0:T(8,128)}) custom-call(s32[2,5]{1,0:T(2,128)} %copy.52.meta, bf16[128,12288]{1,0:T(8,128)(2,1)} %q_ref.1, bf16[128,8192]{1,0:T(8,128)(2,1)} %cot_ref.1, bf16[2,64,32,128]{3,2,1,0:T(8,128)(2,1)} %pad_maximum_fusion.w_ref, ...), custom_call_target="tpu_custom_call" | custom-call | tf_op jit(solution)/shard_map/pallas_call | solution.py:284
  177.1 1.1 convert_element_type.36
  178.2 0.3 convert_element_type.37
  178.6 4.0 %all_to_all.29 = bf16[2,2,96,288]{3,2,1,0:T(8,128)(2,1)S(1)} all-to-all(bf16[2,2,96,288]{3,2,1,0:T(8,128)(2,1)S(1)} %bitcast.47), channel_id=1, replica_groups=mesh['resp'=16,'head'=2] {'head'}, dimensions={0} | all-to-all | bytes 442368 | tf_op jit(solution)/shard_map/all_to_all | solution.py:362
  182.5 0.0 copy-start
  182.6 14.0 %all_to_all.30 = bf16[1,2,32,288]{3,1,0,2:T(2,128)(2,1)S(1)} all-to-all(bf16[1,2,32,288]{3,1,0,2:T(2,128)(2,1)S(1)} %copy.46), channel_id=1, replica_groups=mesh['resp'=16,'head'=2] {'resp'}, dimensions={2} | all-to-all | bytes 73728 | tf_op jit(solution)/shard_map/all_to_all | solution.py:366
  196.6 0.1 reshape.215
  196.7 0.1 dot_general.8
  196.9 0.1 convolution_convert_fusion
  197.0 0.6 copy.49
  197.6 3.5 %all-to-all-start.2 = ((bf16[16,2,288]{2,1,0:T(2,128)(2,1)}), bf16[16,2,288]{2,1,0:T(2,128)(2,1)S(1)}, u32[]{:S(2)}, u32[]{:S(2)}) async-start(bf16[16,2,288]{2,1,0:T(2,128)(2,1)} %copy.49), calls=%async_computation.2 | async-start | bytes 49152 | tf_op jit(solution)/shard_map/all_to_all | solution.py:375
  201.1 0.7 slice.9
  201.8 1.7 copy.50
  203.5 5.0 %all-to-all-done.2 = bf16[16,2,288]{2,1,0:T(2,128)(2,1)S(1)} async-done(((bf16[16,2,288]{2,1,0:T(2,128)(2,1)}), bf16[16,2,288]{2,1,0:T(2,128)(2,1)S(1)}, u32[]{:S(2)}, u32[]{:S(2)}) %all-to-all-start.2) | async-done | bytes 18464 | tf_op jit(solution)/shard_map/all_to_all | solution.py:375
  208.5 0.6 reshape.216
  209.1 3.1 %copy.59 = bf16[128,8192]{1,0:T(8,128)(2,1)} copy(bf16[128,8192]{1,0:T(8,128)(2,1)} %get-tuple-element.31) | data formatting | bytes 4194304
  212.2 0.0 copy-done
  212.2 1.7 copy.60
  (7 shorter events, 0.2 us)
Async XLA Ops:
  182.5 29.7 %copy-start = (bf16[128,12288]{1,0:T(8,128)(2,1)S(1)}, bf16[128,12288]{1,0:T(8,128)(2,1)}, u32[]{:S(2)}) copy-start(bf16[128,12288]{1,0:T(8,128)(2,1)} %get-tuple-element.32) | copy-start | bytes 9437188
  197.6 10.8 %all-to-all-start.2 = ((bf16[16,2,288]{2,1,0:T(2,128)(2,1)}), bf16[16,2,288]{2,1,0:T(2,128)(2,1)S(1)}, u32[]{:S(2)}, u32[]{:S(2)}) async-start(bf16[16,2,288]{2,1,0:T(2,128)(2,1)} %copy.49), calls=%async_computation.2 | async-start | bytes 49152 | tf_op jit(solution)/shard_map/all_to_all | solution.py:375
where the time goes:
time: 214 us
  Pallas kernels  169 us (79%)
  blocking collectives  17.9 us (8%)
  local copies, waits for them, and re-layouts  12.2 us (6%)
  other arithmetic  5.73 us (3%)
  waiting for transfers between devices  4.95 us (2%)
  starting transfers between devices  3.5 us (2%)
    pallas_call x1, Pallas kernels, fused(): pl.pallas_call(functools.partial(kernel, line, chunks, heads_per, resp_pe...  169 us
    all_to_all x1, blocking collectives, body(): lax.all_to_all(grad_prompt_rows[None], 'resp', split_axis=2, concat_axis=...  14 us
    unnamed x7, local copies, waits for them, and re-layouts  8.82 us
    all_to_all x1, waiting for transfers between devices, body(): lax.all_to_all(summed.astype(jnp.bfloat16), 'resp', split_axis=0, concat_...  4.95 us
  transfers between devices with their start and end apart: 1, of which 1 were waited for; matrix products, arithmetic and copies ran while one was open for 1% of the time, Pallas kernels for 0%

commit v1 on v0

--- a/solution.py
+++ b/solution.py
@@ -31,6 +31,7 @@
     resp_ref,
     att_ref,
     gq_ref,
+    parts_ref,
     gk_ref,
     full,
     prompts,
@@ -254,6 +255,14 @@
         for d in range(1, line):
             line_copy(c, d, z).wait_send()
 
+    @pl.when(step == chunks + 2)
+    def _():
+        share = parts_ref.shape[3]
+        for r in range(resp_per):
+            for part in range(parts_ref.shape[0]):
+                cut = gk_ref[r, :, part * share : (part + 1) * share]
+                parts_ref[part, r] = cut.astype(jnp.bfloat16)
+
     @pl.when(step == 3)
     def _():
         sends = prompt_pairs(y, x)
@@ -263,7 +272,7 @@
             line_prompt(d, z).wait_send()
 
 
-def fused(queries, cotangent, weights, prompt_latent, own_rows, meta, resp_devices):
+def fused(queries, cotangent, weights, prompt_latent, own_rows, meta, resp_devices, head_devices):
     line = resp_devices // 4
     head_count, slice_cols, nope = weights.shape[1:]
     resp_per, tokens, key_cols = own_rows.shape
@@ -286,7 +295,9 @@
         out_shape=(
             jax.ShapeDtypeStruct(cotangent.shape, bf),
             jax.ShapeDtypeStruct(queries.shape, bf),
-            jax.ShapeDtypeStruct((resp_per, key_count, key_cols), jnp.float32),
+            jax.ShapeDtypeStruct(
+                (head_devices, resp_per, key_count, key_cols // head_devices), bf
+            ),
         ),
         grid=(chunks + 3,),
         in_specs=[
@@ -303,6 +314,7 @@
             whole,
         ),
         scratch_shapes=[
+            pltpu.VMEM((resp_per, key_count, key_cols), jnp.float32),
             pltpu.VMEM((2, line, 2, 2, head_count, slice_cols, nope), bf),
             pltpu.VMEM((line, 2, 2, prompt_rows, key_cols), bf),
             pltpu.VMEM((resp_per, key_count, key_cols), bf),
@@ -320,6 +332,143 @@
             collective_id=0, has_side_effects=True, dimension_semantics=("arbitrary",)
         ),
     )(meta, queries, cotangent, weights, prompt_latent, own_rows)
+
+
+def tail_kernel(
+    devices,
+    head_devices,
+    prompt_rows,
+    slots,
+    parts_ref,
+    own_ref,
+    prompt_out,
+    head_in,
+    out_rows,
+    in_rows,
+    out_sums,
+    in_sums,
+    head_send,
+    head_recv,
+    row_send,
+    row_recv,
+    sum_send,
+    sum_recv,
+):
+    me = lax.axis_index("resp")
+    mine = lax.axis_index("head")
+    resp_per, key_count, share = parts_ref.shape[1:]
+    tokens = key_count - prompt_rows
+    piece = prompt_rows // devices
+
+    def ahead(d):
+        return lax.rem(me + d, devices)
+
+    def behind(d):
+        return lax.rem(me + devices - d, devices)
+
+    barrier = pltpu.get_barrier_semaphore()
+    for d in range(1, devices):
+        pl.semaphore_signal(barrier, inc=1, device_id={"resp": ahead(d)}, device_id_type=MESH)
+    for d in range(1, head_devices):
+        peer = lax.rem(mine + d, head_devices)
+        pl.semaphore_signal(barrier, inc=1, device_id={"head": peer}, device_id_type=MESH)
+    pl.semaphore_wait(barrier, devices + head_devices - 2)
+
+    def head_copy(d, slot):
+        peer = lax.rem(mine + d, head_devices)
+        return pltpu.make_async_remote_copy(
+            src_ref=parts_ref.at[peer],
+            dst_ref=head_in.at[slot],
+            send_sem=head_send.at[d - 1],
+            recv_sem=head_recv.at[d - 1],
+            device_id={"head": peer},
+            device_id_type=MESH,
+        )
+
+    def spread(source, target, send, recv, d, slot):
+        return pltpu.make_async_remote_copy(
+            src_ref=source.at[ahead(d)],
+            dst_ref=target.at[slot],
+            send_sem=send.at[d - 1],
+            recv_sem=recv.at[d - 1],
+            device_id={"resp": ahead(d)},
+            device_id_type=MESH,
+        )
+
+    for d in range(1, head_devices):
+        head_copy(d, mine).start()
+    total = parts_ref[mine].astype(jnp.float32)
+    for d in range(1, head_devices):
+        source = lax.rem(mine + head_devices - d, head_devices)
+        head_copy(d, source).wait_recv()
+        total = total + head_in[source].astype(jnp.float32)
+    for r in range(resp_per):
+        for i in range(devices):
+            out_rows[i, r * piece : (r + 1) * piece, :] = total[r, i * piece : (i + 1) * piece]
+    for d in range(1, devices):
+        spread(out_rows, in_rows, row_send, row_recv, d, me).start()
+    in_rows[me] = out_rows[me]
+    for r in range(resp_per):
+        own_ref[r * tokens : (r + 1) * tokens, :] = total[r, prompt_rows:]
+    for d in range(1, devices):
+        spread(out_rows, in_rows, row_send, row_recv, d, behind(d)).wait_recv()
+    slot_at = lax.broadcasted_iota(jnp.int32, (devices, devices), 0)
+    for p in range(piece):
+        summed = jnp.zeros((devices, share), jnp.float32)
+        for r in range(resp_per):
+            table = (slot_at == slots[r : r + 1, :]).astype(jnp.float32)
+            summed = summed + lax.dot_general(
+                table,
+                in_rows[:, r * piece + p, :],
+                NN,
+                precision=lax.Precision.HIGHEST,
+                preferred_element_type=jnp.float32,
+            )
+        out_sums[:, p, :] = summed
+    for d in range(1, devices):
+        spread(out_sums, in_sums, sum_send, sum_recv, d, me).start()
+    in_sums[me] = out_sums[me]
+    for d in range(1, devices):
+        spread(out_sums, in_sums, sum_send, sum_recv, d, behind(d)).wait_recv()
+    for i in range(devices):
+        prompt_out[0, i * piece : (i + 1) * piece, :] = in_sums[i]
+    for d in range(1, head_devices):
+        head_copy(d, mine).wait_send()
+    for d in range(1, devices):
+        spread(out_rows, in_rows, row_send, row_recv, d, me).wait_send()
+        spread(out_sums, in_sums, sum_send, sum_recv, d, me).wait_send()
+
+
+def finish(parts, slots, resp_devices, prompt_rows):
+    head_devices, resp_per, key_count, share = parts.shape
+    piece = prompt_rows // resp_devices
+    whole = pl.BlockSpec(memory_space=pltpu.VMEM)
+    spread = pltpu.SemaphoreType.DMA((resp_devices - 1,))
+    across = pltpu.SemaphoreType.DMA((max(head_devices - 1, 1),))
+    f32 = jnp.float32
+    return pl.pallas_call(
+        functools.partial(tail_kernel, resp_devices, head_devices, prompt_rows),
+        out_shape=(
+            jax.ShapeDtypeStruct((resp_per * (key_count - prompt_rows), share), f32),
+            jax.ShapeDtypeStruct((1, prompt_rows, share), f32),
+        ),
+        in_specs=[whole, whole],
+        out_specs=(whole, whole),
+        scratch_shapes=[
+            pltpu.VMEM(parts.shape, parts.dtype),
+            pltpu.VMEM((resp_devices, resp_per * piece, share), f32),
+            pltpu.VMEM((resp_devices, resp_per * piece, share), f32),
+            pltpu.VMEM((resp_devices, piece, share), f32),
+            pltpu.VMEM((resp_devices, piece, share), f32),
+            across,
+            across,
+            spread,
+            spread,
+            spread,
+            spread,
+        ],
+        compiler_params=pltpu.CompilerParams(collective_id=1, has_side_effects=True),
+    )(slots, parts)
 
 
 def body(
@@ -341,9 +490,10 @@
     per_device = resp_total // resp_devices
     row_count = queries.shape[0] // per_device
     prompt_rows = prompt_latent.shape[1]
-    piece_rows = prompt_rows // resp_devices
     latent_cols = prompt_latent.shape[2]
-    starts = jnp.cumsum(resp_count) - resp_count
+    prompts = jnp.arange(resp_count.shape[0], dtype=jnp.int32)
+    earlier = prompts[None, :] < prompts[:, None]
+    starts = jnp.sum(jnp.where(earlier, resp_count[None, :], 0), axis=1)
     numbers = jnp.arange(resp_total, dtype=jnp.int32)
     prompt_of = jnp.sum((starts[None, :] <= numbers[:, None]).astype(jnp.int32), axis=1) - 1
     chosen = prompt_of[:, None] == jnp.arange(prompt_len.shape[0], dtype=jnp.int32)[None, :]
@@ -353,28 +503,11 @@
     meta = lax.dynamic_slice_in_dim(table, my_index * per_device, per_device)
     weights = jnp.stack([jnp.swapaxes(up_keys, 1, 2), up_values])
     own_rows = resp_latent.reshape(per_device, row_count, latent_cols)
-    attended, grad_query, grad_key = fused(
-        queries, cotangent, weights, prompt_latent, own_rows, meta, resp_devices
+    attended, grad_query, parts = fused(
+        queries, cotangent, weights, prompt_latent, own_rows, meta, resp_devices, head_devices
     )
-    share = latent_cols // head_devices
-    parts = grad_key.reshape(per_device, prompt_rows + row_count, head_devices, share)
-    parts = jnp.moveaxis(parts, 2, 0).astype(jnp.bfloat16)
-    parts = lax.all_to_all(parts, "head", split_axis=0, concat_axis=0, tiled=True)
-    mine = jnp.sum(parts.astype(jnp.float32), axis=0)
-    grad_own = mine[:, prompt_rows:].reshape(per_device * row_count, share)
-    grad_prompt_rows = mine[:, :prompt_rows].astype(jnp.bfloat16)
-    arrived = lax.all_to_all(
-        grad_prompt_rows[None], "resp", split_axis=2, concat_axis=0, tiled=True
-    ).astype(jnp.float32)
-    flat_rows = arrived.reshape(resp_devices * per_device, piece_rows * share)
-    slot_table = (slot_of[None, :] == jnp.arange(resp_devices, dtype=jnp.int32)[:, None]).astype(
-        jnp.float32
-    )
-    summed = jnp.dot(slot_table, flat_rows, precision=lax.Precision.HIGHEST)
-    summed = summed.reshape(resp_devices, piece_rows, share)
-    at_owner = lax.all_to_all(
-        summed.astype(jnp.bfloat16), "resp", split_axis=0, concat_axis=1, tiled=True
-    ).astype(summed.dtype)
+    slots = slot_of.reshape(resp_devices, per_device).T
+    grad_own, at_owner = finish(parts, slots, resp_devices, prompt_rows)
     return attended, grad_query, grad_own, at_owner
 
 

time: 214 us -> 202 us (0.944)
  blocking collectives: 17.9 us -> 0 us
  Pallas kernels: 169 us -> 186 us
  waiting for transfers between devices: 4.95 us -> 0 us
  starting transfers between devices: 3.5 us -> 0 us
    all_to_all x2 -> x0, blocking collectives: 17.9 us -> none  [the longest x1 14 us: body(): lax.all_to_all(grad_prompt_rows[None], 'resp', split_axis=2, concat_axis=...]
    pallas_call x0 -> x1, Pallas kernels: none -> 17.6 us  [finish(): pl.pallas_call(functools.partial(tail_kernel, resp_devices, head_devices,...]
    all_to_all x1 -> x0, waiting for transfers between devices: 4.95 us -> none  [body(): lax.all_to_all(summed.astype(jnp.bfloat16), 'resp', split_axis=0, concat_...]
    all_to_all x1 -> x0, starting transfers between devices: 3.5 us -> none  [body(): lax.all_to_all(summed.astype(jnp.bfloat16), 'resp', split_axis=0, concat_...]
    unnamed x7 -> x10, local copies, waits for them, and re-layouts: 8.82 us -> 9.45 us
  transfers between devices with their start and end apart: 1 -> 0, of which waited for: 1 -> 0; matrix products, arithmetic and copies ran while one was open for 1% -> 0% of each run, Pallas kernels for 0% -> 0%
where the time goes in v1:
time: 202 us
  Pallas kernels  186 us (92%)
  local copies, waits for them, and re-layouts  10.9 us (5%)
  other arithmetic  3.91 us (2%)
    pallas_call x1, Pallas kernels, fused(): pl.pallas_call(functools.partial(kernel, line, chunks, heads_per, resp_pe...  169 us
    pallas_call x1, Pallas kernels, finish(): pl.pallas_call(functools.partial(tail_kernel, resp_devices, head_devices,...  17.6 us
    unnamed x10, local copies, waits for them, and re-layouts  9.45 us

profile of v1, /device:TPU:0, one launch (start us, length us, event | category | flops | bytes accessed | tf_op | source)
XLA Modules:
  0.0 201.9 jit_solution(36415975301016913)
XLA Ops:
  0.6 0.8 select_reduce_fusion.2
  1.4 0.1 convert_reduce_fusion
  1.5 0.8 select_reduce_fusion
  2.3 0.7 stack.23
  3.0 0.1 constant_dynamic-slice_fusion
  3.0 0.7 copy.40.meta
  3.7 0.1 reshape.161
  3.8 0.6 copy.38
  4.4 1.7 copy.37
  6.1 2.3 %pad_maximum_fusion.w_ref = bf16[2,64,32,128]{3,2,1,0:T(8,128)(2,1)} fusion(bf16[1,64,32,128]{3,2,1,0:T(8,128)(2,1)} %bitcast.29, bf16[1,64,32,128]{3,2,1,0:T(8,128)(2,1)} %bitcast.30), kind=kLoop, calls=%fused_computation | loop fusion | flops 524288 | bytes 2097152 | tf_op jit(solution)/shard_map/stack | solution.py:504
  8.4 168.8 %shard_map.129 = (bf16[128,8192]{1,0:T(8,128)(2,1)}, bf16[128,12288]{1,0:T(8,128)(2,1)}, bf16[2,2,96,288]{3,2,1,0:T(8,128)(2,1)}) custom-call(s32[2,5]{1,0:T(2,128)} %copy.40.meta, bf16[128,12288]{1,0:T(8,128)(2,1)} %q_ref.1, bf16[128,8192]{1,0:T(8,128)(2,1)} %cot_ref.1, bf16[2,64,32,128]{3,2,1,0:T(8,128)(2,1)} %pad_maximum_fusion.w_ref, ...), custom_call_target="tpu_custom_call" | custom-call | tf_op jit(solution)/shard_map/pallas_call | solution.py:293
  177.2 0.0 copy-start
  177.2 17.6 %shard_map.130 = (f32[128,288]{1,0:T(8,128)}, f32[1,32,288]{2,1,0:T(8,128)}) custom-call(s32[2,16]{1,0:T(2,128)} %bitcast.31, bf16[2,2,96,288]{3,2,1,0:T(8,128)(2,1)} %get-tuple-element.11.parts_ref), custom_call_target="tpu_custom_call" | custom-call | tf_op jit(solution)/shard_map/pallas_call | solution.py:449
  194.8 1.7 copy.39
  196.5 3.1 %copy.44 = bf16[128,8192]{1,0:T(8,128)(2,1)} copy(bf16[128,8192]{1,0:T(8,128)(2,1)} %get-tuple-element.39) | data formatting | bytes 4194304
  199.6 0.0 copy-done
  199.6 0.0 copy-start.1
  199.6 1.7 copy.45
  201.3 0.0 copy-done.1
  201.3 0.6 copy.46
  (2 shorter events, 0.0 us)
Async XLA Ops:
  177.2 22.4 %copy-start = (bf16[128,12288]{1,0:T(8,128)(2,1)S(1)}, bf16[128,12288]{1,0:T(8,128)(2,1)}, u32[]{:S(2)}) copy-start(bf16[128,12288]{1,0:T(8,128)(2,1)} %get-tuple-element.40) | copy-start | bytes 9437188
  199.6 1.7 copy-start.1

commit v2 on v1

--- a/solution.py
+++ b/solution.py
@@ -45,8 +45,12 @@
     line_recv,
     pair_send,
     pair_recv,
+    lead_send,
+    lead_recv,
 ):
     step = pl.program_id(0)
+    ahead = line - 2
+    lag = line + 1
     me = lax.axis_index("resp")
     x = lax.rem(me, 2)
     y = lax.rem(lax.div(me, 2), 2)
@@ -65,6 +69,12 @@
     def heads(c):
         return pl.ds(c * heads_per, heads_per)
 
+    def lead(c):
+        return pl.ds(c * heads_per, 1)
+
+    def rest(c):
+        return pl.ds(c * heads_per + 1, heads_per - 1)
+
     def own_copy(c):
         return pltpu.make_async_copy(
             w_ref.at[:, heads(c)], full.at[:, z, y, x, heads(c)], own_sem.at[c]
@@ -72,18 +82,18 @@
 
     def line_copy(c, d, source):
         return remote(
-            w_ref.at[:, heads(c)],
-            full.at[:, source, y, x, heads(c)],
+            w_ref.at[:, rest(c)],
+            full.at[:, source, y, x, rest(c)],
             line_send.at[c, d - 1],
             line_recv.at[c, d - 1],
             at(lax.rem(z + d, line), y, x),
         )
 
     def pair_copies(c, yy, xx):
-        first_k = full.at[0, :, yy[0], xx[0], heads(c)]
-        first_v = full.at[1, :, yy[1], xx[1], heads(c)]
-        second_k = full.at[0, :, :, xx[2], heads(c)]
-        second_v = full.at[1, :, yy[2], :, heads(c)]
+        first_k = full.at[0, :, yy[0], xx[0], rest(c)]
+        first_v = full.at[1, :, yy[1], xx[1], rest(c)]
+        second_k = full.at[0, :, :, xx[2], rest(c)]
+        second_v = full.at[1, :, yy[2], :, rest(c)]
         refs = ((first_k, y_peer), (first_v, x_peer), (second_k, x_peer), (second_v, y_peer))
         return [
             remote(ref, ref, pair_send.at[c, i], pair_recv.at[c, i], peer)
@@ -95,6 +105,42 @@
 
     def in_pairs(c):
         return pair_copies(c, (1 - y, y, 1 - y), (x, 1 - x, 1 - x))
+
+    def lead_x(c, xx):
+        ref = full.at[:, z, y, xx, lead(c)]
+        return remote(w_ref.at[:, lead(c)], ref, lead_send.at[c, 0], lead_recv.at[c, 0], x_peer)
+
+    def lead_y(c, yy):
+        ref = full.at[:, z, yy, :, lead(c)]
+        return remote(ref, ref, lead_send.at[c, 1], lead_recv.at[c, 1], y_peer)
+
+    def lead_up(c, j, source):
+        ref = full.at[:, source, :, :, lead(c)]
+        k = 2 * j
+        return remote(ref, ref, lead_send.at[c, k], lead_recv.at[c, k], at(z + 1, y, x))
+
+    def lead_down(c, j, source):
+        ref = full.at[:, source, :, :, lead(c)]
+        k = 2 * j + 1
+        return remote(ref, ref, lead_send.at[c, k], lead_recv.at[c, k], at(z - 1, y, x))
+
+    def lead_arrived(c, j):
+        @pl.when(z >= j)
+        def _():
+            lead_up(c, j, z - j).wait_recv()
+
+        @pl.when(z + j < line)
+        def _():
+            lead_down(c, j, z + j).wait_recv()
+
+    def lead_onward(c, j, act):
+        @pl.when((z + 1 >= j) & (z + 1 < line))
+        def _():
+            act(lead_up(c, j, z - j + 1))
+
+        @pl.when((z >= 1) & (z + j - 1 < line))
+        def _():
+            act(lead_down(c, j, z + j - 1))
 
     def own_prompt():
         return pltpu.make_async_copy(prompt_ref.at[0], prompts.at[z, y, x], own_sem.at[chunks])
@@ -130,11 +176,40 @@
             line_prompt(d, z).start()
         gk_ref[...] = jnp.zeros_like(gk_ref)
 
-    @pl.when(step < chunks)
+    def during(delay):
+        return pl.when((step >= delay) & (step < chunks + delay))
+
+    @during(0)
     def _():
         own_copy(step).start()
+        lead_x(step, x).start()
+
+    @during(ahead)
+    def _():
+        c = step - ahead
         for d in range(1, line):
-            line_copy(step, d, z).start()
+            line_copy(c, d, z).start()
+
+    @during(1)
+    def _():
+        c = step - 1
+        own_copy(c).wait()
+        lead_x(c, 1 - x).wait_recv()
+        lead_y(c, y).start()
+
+    @during(2)
+    def _():
+        c = step - 2
+        lead_y(c, 1 - y).wait_recv()
+        lead_onward(c, 1, lambda copy: copy.start())
+
+    for hop in range(2, line):
+
+        @during(1 + hop)
+        def _(hop=hop):
+            c = step - 1 - hop
+            lead_arrived(c, hop - 1)
+            lead_onward(c, hop, lambda copy: copy.start())
 
     @pl.when(step == 1)
     def _():
@@ -143,10 +218,9 @@
             line_prompt(d, lax.rem(z + line - d, line)).wait_recv()
         prompt_pairs(y, x)[0].start()
 
-    @pl.when((step >= 1) & (step < chunks + 1))
-    def _():
-        c = step - 1
-        own_copy(c).wait()
+    @during(ahead + 1)
+    def _():
+        c = step - ahead - 1
         for d in range(1, line):
             line_copy(c, d, lax.rem(z + line - d, line)).wait_recv()
         sends = out_pairs(c)
@@ -158,9 +232,9 @@
         prompt_pairs(1 - y, 1 - x)[0].wait_recv()
         prompt_pairs(y, x)[1].start()
 
-    @pl.when((step >= 2) & (step < chunks + 2))
-    def _():
-        c = step - 2
+    @during(ahead + 2)
+    def _():
+        c = step - ahead - 2
         arrivals, sends = in_pairs(c), out_pairs(c)
         arrivals[0].wait_recv()
         arrivals[1].wait_recv()
@@ -177,16 +251,17 @@
     rows = heads_per * tokens
     scale = 1.0 / math.sqrt(q_cols)
 
-    @pl.when(step == 3)
+    @pl.when(step == lag)
     def _():
         prompt_pairs(1 - y, 1 - x)[1].wait_recv()
         for r in range(resp_per):
             keys[r, :plen_rows, :] = prompts[meta[r, 0], meta[r, 1], meta[r, 2]]
             keys[r, plen_rows:, :] = resp_ref[r]
 
-    @pl.when(step >= 3)
-    def _():
-        c = step - 3
+    @pl.when(step >= lag)
+    def _():
+        c = step - lag
+        lead_arrived(c, line - 1)
         arrivals = in_pairs(c)
         arrivals[2].wait_recv()
         arrivals[3].wait_recv()
@@ -254,8 +329,12 @@
             sends[i].wait_send()
         for d in range(1, line):
             line_copy(c, d, z).wait_send()
-
-    @pl.when(step == chunks + 2)
+        lead_x(c, x).wait_send()
+        lead_y(c, y).wait_send()
+        for hop in range(1, line):
+            lead_onward(c, hop, lambda copy: copy.wait_send())
+
+    @pl.when(step == chunks + lag - 1)
     def _():
         share = parts_ref.shape[3]
         for r in range(resp_per):
@@ -263,7 +342,7 @@
                 cut = gk_ref[r, :, part * share : (part + 1) * share]
                 parts_ref[part, r] = cut.astype(jnp.bfloat16)
 
-    @pl.when(step == 3)
+    @pl.when(step == lag)
     def _():
         sends = prompt_pairs(y, x)
         sends[0].wait_send()
@@ -287,7 +366,7 @@
     bf = jnp.bfloat16
 
     def tile(t):
-        return (0, lax.max(t - 3, 0))
+        return (0, lax.max(t - line - 1, 0))
 
     whole = pl.BlockSpec(memory_space=pltpu.VMEM)
     return pl.pallas_call(
@@ -299,7 +378,7 @@
                 (head_devices, resp_per, key_count, key_cols // head_devices), bf
             ),
         ),
-        grid=(chunks + 3,),
+        grid=(chunks + line + 1,),
         in_specs=[
             pl.BlockSpec(memory_space=pltpu.SMEM),
             pl.BlockSpec((row_count, heads_per * q_cols), tile),
@@ -327,6 +406,8 @@
             pltpu.SemaphoreType.DMA((chunks + 1, line - 1)),
             pltpu.SemaphoreType.DMA((chunks + 1, 4)),
             pltpu.SemaphoreType.DMA((chunks + 1, 4)),
+            pltpu.SemaphoreType.DMA((chunks, 2 * line)),
+            pltpu.SemaphoreType.DMA((chunks, 2 * line)),
         ],
         compiler_params=pltpu.CompilerParams(
             collective_id=0, has_side_effects=True, dimension_semantics=("arbitrary",)

time: 202 us -> 177 us (0.88)
  Pallas kernels: 186 us -> 161 us
    pallas_call x1, Pallas kernels: 169 us -> 146 us  [fused(): pl.pallas_call(functools.partial(kernel, line, chunks, heads_per, resp_pe...]
    pallas_call x1, Pallas kernels: 17.6 us -> 15.1 us  [finish(): pl.pallas_call(functools.partial(tail_kernel, resp_devices, head_devices,...]
where the time goes in v2:
time: 177 us
  Pallas kernels  161 us (91%)
  local copies, waits for them, and re-layouts  10.9 us (6%)
  other arithmetic  3.91 us (2%)
    pallas_call x1, Pallas kernels, fused(): pl.pallas_call(functools.partial(kernel, line, chunks, heads_per, resp_pe...  146 us
    pallas_call x1, Pallas kernels, finish(): pl.pallas_call(functools.partial(tail_kernel, resp_devices, head_devices,...  15.1 us
    unnamed x10, local copies, waits for them, and re-layouts  9.45 us

profile of v2, /device:TPU:0, one launch (start us, length us, event | category | flops | bytes accessed | tf_op | source)
XLA Modules:
  0.0 176.9 jit_solution(17751616609233713079)
XLA Ops:
  0.6 0.8 select_reduce_fusion.2
  1.4 0.1 convert_reduce_fusion
  1.5 0.8 select_reduce_fusion
  2.3 0.7 stack.23
  3.0 0.1 constant_dynamic-slice_fusion
  3.0 0.7 copy.40.meta
  3.7 0.1 reshape.161
  3.8 0.6 copy.38
  4.4 1.7 copy.37
  6.1 2.3 %pad_maximum_fusion.w_ref = bf16[2,64,32,128]{3,2,1,0:T(8,128)(2,1)} fusion(bf16[1,64,32,128]{3,2,1,0:T(8,128)(2,1)} %bitcast.29, bf16[1,64,32,128]{3,2,1,0:T(8,128)(2,1)} %bitcast.30), kind=kLoop, calls=%fused_computation | loop fusion | flops 524288 | bytes 2097152 | tf_op jit(solution)/shard_map/stack | solution.py:585
  8.4 146.3 %shard_map.129 = (bf16[128,8192]{1,0:T(8,128)(2,1)}, bf16[128,12288]{1,0:T(8,128)(2,1)}, bf16[2,2,96,288]{3,2,1,0:T(8,128)(2,1)}) custom-call(s32[2,5]{1,0:T(2,128)} %copy.40.meta, bf16[128,12288]{1,0:T(8,128)(2,1)} %q_ref.1, bf16[128,8192]{1,0:T(8,128)(2,1)} %cot_ref.1, bf16[2,64,32,128]{3,2,1,0:T(8,128)(2,1)} %pad_maximum_fusion.w_ref, ...), custom_call_target="tpu_custom_call" | custom-call | tf_op jit(solution)/shard_map/pallas_call | solution.py:372
  154.7 0.0 copy-start
  154.7 15.1 %shard_map.130 = (f32[128,288]{1,0:T(8,128)}, f32[1,32,288]{2,1,0:T(8,128)}) custom-call(s32[2,16]{1,0:T(2,128)} %bitcast.31, bf16[2,2,96,288]{3,2,1,0:T(8,128)(2,1)} %get-tuple-element.11.parts_ref), custom_call_target="tpu_custom_call" | custom-call | tf_op jit(solution)/shard_map/pallas_call | solution.py:530
  169.8 1.7 copy.39
  171.5 3.1 %copy.44 = bf16[128,8192]{1,0:T(8,128)(2,1)} copy(bf16[128,8192]{1,0:T(8,128)(2,1)} %get-tuple-element.39) | data formatting | bytes 4194304
  174.6 0.0 copy-done
  174.6 0.0 copy-start.1
  174.6 1.7 copy.45
  176.2 0.0 copy-done.1
  176.2 0.6 copy.46
  (2 shorter events, 0.0 us)
Async XLA Ops:
  154.7 19.9 %copy-start = (bf16[128,12288]{1,0:T(8,128)(2,1)S(1)}, bf16[128,12288]{1,0:T(8,128)(2,1)}, u32[]{:S(2)}) copy-start(bf16[128,12288]{1,0:T(8,128)(2,1)} %get-tuple-element.40) | copy-start | bytes 9437188
  174.6 1.7 copy-start.1

commit v3 on v2

--- a/solution.py
+++ b/solution.py
@@ -26,7 +26,8 @@
     meta,
     q_ref,
     cot_ref,
-    w_ref,
+    wk_ref,
+    wv_ref,
     prompt_ref,
     resp_ref,
     att_ref,
@@ -49,7 +50,8 @@
     lead_recv,
 ):
     step = pl.program_id(0)
-    ahead = line - 2
+    ahead = max(line - 3, 0)
+    leads = chunks - chunks // 8
     lag = line + 1
     me = lax.axis_index("resp")
     x = lax.rem(me, 2)
@@ -75,40 +77,42 @@
     def rest(c):
         return pl.ds(c * heads_per + 1, heads_per - 1)
 
-    def own_copy(c):
-        return pltpu.make_async_copy(
-            w_ref.at[:, heads(c)], full.at[:, z, y, x, heads(c)], own_sem.at[c]
-        )
-
-    def line_copy(c, d, source):
+    def own_copies():
+        return [
+            pltpu.make_async_copy(ref, full.at[kind, z, y, x], own_sem.at[kind])
+            for kind, ref in enumerate((wk_ref, wv_ref))
+        ]
+
+    def line_copy(c, d, source, span):
         return remote(
-            w_ref.at[:, rest(c)],
-            full.at[:, source, y, x, rest(c)],
+            full.at[:, z, y, x, span],
+            full.at[:, source, y, x, span],
             line_send.at[c, d - 1],
             line_recv.at[c, d - 1],
             at(lax.rem(z + d, line), y, x),
         )
 
-    def pair_copies(c, yy, xx):
-        first_k = full.at[0, :, yy[0], xx[0], rest(c)]
-        first_v = full.at[1, :, yy[1], xx[1], rest(c)]
-        second_k = full.at[0, :, :, xx[2], rest(c)]
-        second_v = full.at[1, :, yy[2], :, rest(c)]
+    def pair_copies(c, yy, xx, span):
+        first_k = full.at[0, :, yy[0], xx[0], span]
+        first_v = full.at[1, :, yy[1], xx[1], span]
+        second_k = full.at[0, :, :, xx[2], span]
+        second_v = full.at[1, :, yy[2], :, span]
         refs = ((first_k, y_peer), (first_v, x_peer), (second_k, x_peer), (second_v, y_peer))
         return [
             remote(ref, ref, pair_send.at[c, i], pair_recv.at[c, i], peer)
             for i, (ref, peer) in enumerate(refs)
         ]
 
-    def out_pairs(c):
-        return pair_copies(c, (y, y, y), (x, x, x))
-
-    def in_pairs(c):
-        return pair_copies(c, (1 - y, y, 1 - y), (x, 1 - x, 1 - x))
+    def out_pairs(c, span):
+        return pair_copies(c, (y, y, y), (x, x, x), span)
+
+    def in_pairs(c, span):
+        return pair_copies(c, (1 - y, y, 1 - y), (x, 1 - x, 1 - x), span)
 
     def lead_x(c, xx):
         ref = full.at[:, z, y, xx, lead(c)]
-        return remote(w_ref.at[:, lead(c)], ref, lead_send.at[c, 0], lead_recv.at[c, 0], x_peer)
+        own = full.at[:, z, y, x, lead(c)]
+        return remote(own, ref, lead_send.at[c, 0], lead_recv.at[c, 0], x_peer)
 
     def lead_y(c, yy):
         ref = full.at[:, z, yy, :, lead(c)]
@@ -143,7 +147,7 @@
             act(lead_down(c, j, z + j - 1))
 
     def own_prompt():
-        return pltpu.make_async_copy(prompt_ref.at[0], prompts.at[z, y, x], own_sem.at[chunks])
+        return pltpu.make_async_copy(prompt_ref.at[0], prompts.at[z, y, x], own_sem.at[2])
 
     def line_prompt(d, source):
         return remote(
@@ -163,6 +167,8 @@
 
     @pl.when(step == 0)
     def _():
+        for copy in own_copies():
+            copy.start()
         barrier = pltpu.get_barrier_semaphore()
         for d in range(1, line):
             pl.semaphore_signal(
@@ -175,29 +181,42 @@
         for d in range(1, line):
             line_prompt(d, z).start()
         gk_ref[...] = jnp.zeros_like(gk_ref)
-
-    def during(delay):
-        return pl.when((step >= delay) & (step < chunks + delay))
-
-    @during(0)
-    def _():
-        own_copy(step).start()
+        for copy in own_copies():
+            copy.wait()
+
+    def during(delay, count):
+        return pl.when((step >= delay) & (step < count + delay))
+
+    def spanned(c, act):
+        @pl.when(c < leads)
+        def _():
+            act(rest(c))
+
+        @pl.when(c >= leads)
+        def _():
+            act(heads(c))
+
+    @during(0, leads)
+    def _():
         lead_x(step, x).start()
 
-    @during(ahead)
+    @during(ahead, chunks)
     def _():
         c = step - ahead
-        for d in range(1, line):
-            line_copy(c, d, z).start()
-
-    @during(1)
+
+        def act(span):
+            for d in range(1, line):
+                line_copy(c, d, z, span).start()
+
+        spanned(c, act)
+
+    @during(1, leads)
     def _():
         c = step - 1
-        own_copy(c).wait()
         lead_x(c, 1 - x).wait_recv()
         lead_y(c, y).start()
 
-    @during(2)
+    @during(2, leads)
     def _():
         c = step - 2
         lead_y(c, 1 - y).wait_recv()
@@ -205,7 +224,7 @@
 
     for hop in range(2, line):
 
-        @during(1 + hop)
+        @during(1 + hop, leads)
         def _(hop=hop):
             c = step - 1 - hop
             lead_arrived(c, hop - 1)
@@ -218,34 +237,42 @@
             line_prompt(d, lax.rem(z + line - d, line)).wait_recv()
         prompt_pairs(y, x)[0].start()
 
-    @during(ahead + 1)
+    @during(ahead + 1, chunks)
     def _():
         c = step - ahead - 1
-        for d in range(1, line):
-            line_copy(c, d, lax.rem(z + line - d, line)).wait_recv()
-        sends = out_pairs(c)
-        sends[0].start()
-        sends[1].start()
+
+        def act(span):
+            for d in range(1, line):
+                line_copy(c, d, lax.rem(z + line - d, line), span).wait_recv()
+            sends = out_pairs(c, span)
+            sends[0].start()
+            sends[1].start()
+
+        spanned(c, act)
 
     @pl.when(step == 2)
     def _():
         prompt_pairs(1 - y, 1 - x)[0].wait_recv()
         prompt_pairs(y, x)[1].start()
 
-    @during(ahead + 2)
+    @during(ahead + 2, chunks)
     def _():
         c = step - ahead - 2
-        arrivals, sends = in_pairs(c), out_pairs(c)
-        arrivals[0].wait_recv()
-        arrivals[1].wait_recv()
-        sends[2].start()
-        sends[3].start()
+
+        def act(span):
+            arrivals, sends = in_pairs(c, span), out_pairs(c, span)
+            arrivals[0].wait_recv()
+            arrivals[1].wait_recv()
+            sends[2].start()
+            sends[3].start()
+
+        spanned(c, act)
 
     plen_rows = prompt_ref.shape[1]
     tokens = resp_ref.shape[1]
     key_count, key_cols = keys.shape[1], keys.shape[2]
     latent = gl.shape[2]
-    slice_cols, nope = w_ref.shape[2], w_ref.shape[3]
+    slice_cols, nope = wk_ref.shape[1], wk_ref.shape[2]
     value_cols = nope
     q_cols = q_ref.shape[1] // heads_per
     rows = heads_per * tokens
@@ -261,10 +288,17 @@
     @pl.when(step >= lag)
     def _():
         c = step - lag
-        lead_arrived(c, line - 1)
-        arrivals = in_pairs(c)
-        arrivals[2].wait_recv()
-        arrivals[3].wait_recv()
+
+        @pl.when(c < leads)
+        def _():
+            lead_arrived(c, line - 1)
+
+        def arrive(span):
+            arrivals = in_pairs(c, span)
+            arrivals[2].wait_recv()
+            arrivals[3].wait_recv()
+
+        spanned(c, arrive)
 
         def weight(kind, h):
             got = full[kind, :, :, :, c * heads_per + h]
@@ -324,15 +358,21 @@
             gq_ref[:, h * q_cols : h * q_cols + nope] = grad_nope
             gq_ref[:, h * q_cols + nope : (h + 1) * q_cols] = gf[h, :, latent:]
 
-        sends = out_pairs(c)
-        for i in range(4):
-            sends[i].wait_send()
-        for d in range(1, line):
-            line_copy(c, d, z).wait_send()
-        lead_x(c, x).wait_send()
-        lead_y(c, y).wait_send()
-        for hop in range(1, line):
-            lead_onward(c, hop, lambda copy: copy.wait_send())
+        def settle(span):
+            sends = out_pairs(c, span)
+            for i in range(4):
+                sends[i].wait_send()
+            for d in range(1, line):
+                line_copy(c, d, z, span).wait_send()
+
+        spanned(c, settle)
+
+        @pl.when(c < leads)
+        def _():
+            lead_x(c, x).wait_send()
+            lead_y(c, y).wait_send()
+            for hop in range(1, line):
+                lead_onward(c, hop, lambda copy: copy.wait_send())
 
     @pl.when(step == chunks + lag - 1)
     def _():
@@ -351,9 +391,9 @@
             line_prompt(d, z).wait_send()
 
 
-def fused(queries, cotangent, weights, prompt_latent, own_rows, meta, resp_devices, head_devices):
+def fused(queries, cotangent, wk, wv, prompt_latent, own_rows, meta, resp_devices, head_devices):
     line = resp_devices // 4
-    head_count, slice_cols, nope = weights.shape[1:]
+    head_count, slice_cols, nope = wk.shape
     resp_per, tokens, key_cols = own_rows.shape
     prompt_rows = prompt_latent.shape[1]
     heads_per = math.gcd(4, head_count)
@@ -383,7 +423,8 @@
             pl.BlockSpec(memory_space=pltpu.SMEM),
             pl.BlockSpec((row_count, heads_per * q_cols), tile),
             pl.BlockSpec((row_count, heads_per * nope), tile),
-            whole,
+            pl.BlockSpec(memory_space=pl.ANY),
+            pl.BlockSpec(memory_space=pl.ANY),
             whole,
             whole,
         ],
@@ -401,7 +442,7 @@
             pltpu.VMEM((resp_per, rows, latent), bf),
             pltpu.VMEM((heads_per, resp_per * tokens, latent), bf),
             pltpu.VMEM((heads_per, resp_per * tokens, key_cols), bf),
-            pltpu.SemaphoreType.DMA((chunks + 1,)),
+            pltpu.SemaphoreType.DMA((3,)),
             pltpu.SemaphoreType.DMA((chunks + 1, line - 1)),
             pltpu.SemaphoreType.DMA((chunks + 1, line - 1)),
             pltpu.SemaphoreType.DMA((chunks + 1, 4)),
@@ -412,7 +453,7 @@
         compiler_params=pltpu.CompilerParams(
             collective_id=0, has_side_effects=True, dimension_semantics=("arbitrary",)
         ),
-    )(meta, queries, cotangent, weights, prompt_latent, own_rows)
+    )(meta, queries, cotangent, wk, wv, prompt_latent, own_rows)
 
 
 def tail_kernel(
@@ -582,10 +623,10 @@
     plen_of = jnp.sum(jnp.where(chosen, prompt_len[None, :], 0), axis=1)
     table = jnp.stack([slot_of // 4, (slot_of // 2) % 2, slot_of % 2, plen_of, resp_len], axis=1)
     meta = lax.dynamic_slice_in_dim(table, my_index * per_device, per_device)
-    weights = jnp.stack([jnp.swapaxes(up_keys, 1, 2), up_values])
+    keys_t = jnp.swapaxes(up_keys, 1, 2)
     own_rows = resp_latent.reshape(per_device, row_count, latent_cols)
     attended, grad_query, parts = fused(
-        queries, cotangent, weights, prompt_latent, own_rows, meta, resp_devices, head_devices
+        queries, cotangent, keys_t, up_values, prompt_latent, own_rows, meta, resp_devices, head_devices
     )
     slots = slot_of.reshape(resp_devices, per_device).T
     grad_own, at_owner = finish(parts, slots, resp_devices, prompt_rows)

time: 177 us -> 175 us (0.989)
  other arithmetic: 3.91 us -> 1.64 us
    another operation x1 -> x0, other arithmetic: 2.27 us -> none  [body(): weights = jnp.stack([jnp.swapaxes(up_keys, 1, 2), up_values])]
where the time goes in v3:
time: 175 us
  Pallas kernels  162 us (93%)
  local copies, waits for them, and re-layouts  10.9 us (6%)
    pallas_call x1, Pallas kernels, fused(): pl.pallas_call(functools.partial(kernel, line, chunks, heads_per, resp_pe...  148 us
    pallas_call x1, Pallas kernels, finish(): pl.pallas_call(functools.partial(tail_kernel, resp_devices, head_devices,...  14.4 us
    unnamed x10, local copies, waits for them, and re-layouts  9.45 us

profile of v3, /device:TPU:0, one launch (start us, length us, event | category | flops | bytes accessed | tf_op | source)
XLA Modules:
  0.0 175.3 jit_solution(4558224097829182552)
XLA Ops:
  0.6 0.8 select_reduce_fusion.2
  1.4 0.1 convert_reduce_fusion
  1.5 0.8 select_reduce_fusion
  2.3 0.7 stack.14
  3.0 0.1 constant_dynamic-slice_fusion
  3.0 0.7 copy.40.meta
  3.7 0.1 reshape.161
  3.8 0.6 copy.38
  4.4 1.7 copy.37
  6.1 147.6 %shard_map.129 = (bf16[128,8192]{1,0:T(8,128)(2,1)}, bf16[128,12288]{1,0:T(8,128)(2,1)}, bf16[2,2,96,288]{3,2,1,0:T(8,128)(2,1)}) custom-call(s32[2,5]{1,0:T(2,128)} %copy.40.meta, bf16[128,12288]{1,0:T(8,128)(2,1)} %q_ref.1, bf16[128,8192]{1,0:T(8,128)(2,1)} %cot_ref.1, bf16[64,32,128]{2,1,0:T(8,128)(2,1)} %bitcast.26, bf16[64,32,128]{2,1,0:T(8,128)(2,1)} %wv_ref.1, ...), custom_call_target="tpu_custom_call" | custom-call | tf_op jit(solution)/shard_map/pallas_call | solution.py:412
  153.7 0.0 copy-start
  153.7 14.4 %shard_map.130 = (f32[128,288]{1,0:T(8,128)}, f32[1,32,288]{2,1,0:T(8,128)}) custom-call(s32[2,16]{1,0:T(2,128)} %bitcast.27, bf16[2,2,96,288]{3,2,1,0:T(8,128)(2,1)} %get-tuple-element.11.parts_ref), custom_call_target="tpu_custom_call" | custom-call | tf_op jit(solution)/shard_map/pallas_call | solution.py:571
  168.2 1.7 copy.39
  169.9 3.1 %copy.44 = bf16[128,8192]{1,0:T(8,128)(2,1)} copy(bf16[128,8192]{1,0:T(8,128)(2,1)} %get-tuple-element.39) | data formatting | bytes 4194304
  173.0 0.0 copy-done
  173.0 0.0 copy-start.1
  173.0 1.7 copy.45
  174.6 0.0 copy-done.1
  174.6 0.6 copy.46
  (2 shorter events, 0.0 us)
Async XLA Ops:
  153.7 19.2 %copy-start = (bf16[128,12288]{1,0:T(8,128)(2,1)S(1)}, bf16[128,12288]{1,0:T(8,128)(2,1)}, u32[]{:S(2)}) copy-start(bf16[128,12288]{1,0:T(8,128)(2,1)} %get-tuple-element.40) | copy-start | bytes 9437188
  173.0 1.7 copy-start.1

commit v4 on v3

--- a/solution.py
+++ b/solution.py
@@ -50,8 +50,8 @@
     lead_recv,
 ):
     step = pl.program_id(0)
-    ahead = max(line - 3, 0)
-    leads = chunks - chunks // 8
+    ahead = line - 2
+    leads = chunks
     lag = line + 1
     me = lax.axis_index("resp")
     x = lax.rem(me, 2)
@@ -269,7 +269,7 @@
         spanned(c, act)
 
     plen_rows = prompt_ref.shape[1]
-    tokens = resp_ref.shape[1]
+    tokens = resp_ref.shape[1] // resp_per
     key_count, key_cols = keys.shape[1], keys.shape[2]
     latent = gl.shape[2]
     slice_cols, nope = wk_ref.shape[1], wk_ref.shape[2]
@@ -283,7 +283,8 @@
         prompt_pairs(1 - y, 1 - x)[1].wait_recv()
         for r in range(resp_per):
             keys[r, :plen_rows, :] = prompts[meta[r, 0], meta[r, 1], meta[r, 2]]
-            keys[r, plen_rows:, :] = resp_ref[r]
+            own = resp_ref[:, r * tokens : (r + 1) * tokens].astype(jnp.float32)
+            keys[r, plen_rows:, :] = jnp.transpose(own).astype(jnp.bfloat16)
 
     @pl.when(step >= lag)
     def _():
@@ -391,10 +392,12 @@
             line_prompt(d, z).wait_send()
 
 
-def fused(queries, cotangent, wk, wv, prompt_latent, own_rows, meta, resp_devices, head_devices):
+def fused(queries, cotangent, wk, wv, prompt_latent, own_cols, meta, resp_devices, head_devices):
+    resp_per = meta.shape[0]
     line = resp_devices // 4
     head_count, slice_cols, nope = wk.shape
-    resp_per, tokens, key_cols = own_rows.shape
+    key_cols = own_cols.shape[0]
+    tokens = own_cols.shape[1] // resp_per
     prompt_rows = prompt_latent.shape[1]
     heads_per = math.gcd(4, head_count)
     chunks = head_count // heads_per
@@ -453,7 +456,7 @@
         compiler_params=pltpu.CompilerParams(
             collective_id=0, has_side_effects=True, dimension_semantics=("arbitrary",)
         ),
-    )(meta, queries, cotangent, wk, wv, prompt_latent, own_rows)
+    )(meta, queries, cotangent, wk, wv, prompt_latent, own_cols)
 
 
 def tail_kernel(
@@ -610,9 +613,7 @@
     my_index = lax.axis_index("resp")
     resp_total = resp_len.shape[0]
     per_device = resp_total // resp_devices
-    row_count = queries.shape[0] // per_device
     prompt_rows = prompt_latent.shape[1]
-    latent_cols = prompt_latent.shape[2]
     prompts = jnp.arange(resp_count.shape[0], dtype=jnp.int32)
     earlier = prompts[None, :] < prompts[:, None]
     starts = jnp.sum(jnp.where(earlier, resp_count[None, :], 0), axis=1)
@@ -624,9 +625,9 @@
     table = jnp.stack([slot_of // 4, (slot_of // 2) % 2, slot_of % 2, plen_of, resp_len], axis=1)
     meta = lax.dynamic_slice_in_dim(table, my_index * per_device, per_device)
     keys_t = jnp.swapaxes(up_keys, 1, 2)
-    own_rows = resp_latent.reshape(per_device, row_count, latent_cols)
+    own_cols = resp_latent.T
     attended, grad_query, parts = fused(
-        queries, cotangent, keys_t, up_values, prompt_latent, own_rows, meta, resp_devices, head_devices
+        queries, cotangent, keys_t, up_values, prompt_latent, own_cols, meta, resp_devices, head_devices
     )
     slots = slot_of.reshape(resp_devices, per_device).T
     grad_own, at_owner = finish(parts, slots, resp_devices, prompt_rows)

time: 175 us -> 173 us (0.989)
    pallas_call x1, Pallas kernels: 148 us -> 146 us  [fused(): pl.pallas_call(functools.partial(kernel, line, chunks, heads_per, resp_pe...]
    unnamed x10 -> x9, local copies, waits for them, and re-layouts: 9.45 us -> 7.73 us
where the time goes in v4:
time: 173 us
  Pallas kernels  161 us (93%)
  local copies, waits for them, and re-layouts  9.21 us (5%)
    pallas_call x1, Pallas kernels, fused(): pl.pallas_call(functools.partial(kernel, line, chunks, heads_per, resp_pe...  146 us
    pallas_call x1, Pallas kernels, finish(): pl.pallas_call(functools.partial(tail_kernel, resp_devices, head_devices,...  15.8 us
    unnamed x9, local copies, waits for them, and re-layouts  7.73 us

profile of v4, /device:TPU:0, one launch (start us, length us, event | category | flops | bytes accessed | tf_op | source)
XLA Modules:
  0.0 172.8 jit_solution(14030727666659296815)
XLA Ops:
  0.6 0.8 select_reduce_fusion.2
  1.4 0.1 convert_reduce_fusion
  1.5 0.8 select_reduce_fusion
  2.3 0.7 stack.14
  3.0 0.1 constant_dynamic-slice_fusion
  3.0 0.7 copy.36.meta
  3.7 0.1 reshape.157
  3.8 0.6 copy.34
  4.4 145.5 %shard_map.129 = (bf16[128,8192]{1,0:T(8,128)(2,1)}, bf16[128,12288]{1,0:T(8,128)(2,1)}, bf16[2,2,96,288]{3,2,1,0:T(8,128)(2,1)}) custom-call(s32[2,5]{1,0:T(2,128)} %copy.36.meta, bf16[128,12288]{1,0:T(8,128)(2,1)} %q_ref.1, bf16[128,8192]{1,0:T(8,128)(2,1)} %cot_ref.1, bf16[64,32,128]{2,1,0:T(8,128)(2,1)} %bitcast.25, bf16[64,32,128]{2,1,0:T(8,128)(2,1)} %wv_ref.1, ...), custom_call_target="tpu_custom_call" | custom-call | tf_op jit(solution)/shard_map/pallas_call | solution.py:415
  149.9 0.0 copy-start
  149.9 15.8 %shard_map.130 = (f32[128,288]{1,0:T(8,128)}, f32[1,32,288]{2,1,0:T(8,128)}) custom-call(s32[2,16]{1,0:T(2,128)} %bitcast.27, bf16[2,2,96,288]{3,2,1,0:T(8,128)(2,1)} %get-tuple-element.11.parts_ref), custom_call_target="tpu_custom_call" | custom-call | tf_op jit(solution)/shard_map/pallas_call | solution.py:574
  165.7 1.7 copy.35
  167.4 3.1 %copy.40 = bf16[128,8192]{1,0:T(8,128)(2,1)} copy(bf16[128,8192]{1,0:T(8,128)(2,1)} %get-tuple-element.39) | data formatting | bytes 4194304
  170.5 0.0 copy-done
  170.5 0.0 copy-start.1
  170.5 1.7 copy.41
  172.2 0.0 copy-done.1
  172.2 0.6 copy.42
  (2 shorter events, 0.0 us)
Async XLA Ops:
  149.9 20.6 %copy-start = (bf16[128,12288]{1,0:T(8,128)(2,1)S(1)}, bf16[128,12288]{1,0:T(8,128)(2,1)}, u32[]{:S(2)}) copy-start(bf16[128,12288]{1,0:T(8,128)(2,1)} %get-tuple-element.40) | copy-start | bytes 9437188
  170.5 1.7 copy-start.1
